TPU v7x, 256 devices: a whole 4x4x8 slice. The times are simulated.
256 devices in a mesh: tm: 32 (over x, z), chan: 8 (over y, core).
Axes of the slice: x: 4, y: 4, z: 8, core: 2. Of those that a mesh axis runs over, the one named last changes fastest.
Arguments:
- visibilities: bfloat16 [32, 8, 512, 1024], P('tm', None, None, 'chan'), may hold values from -6 to 6
- station_gains: float32 [8, 192, 1024], P(None, 'chan'), may hold values from -1.5 to 1.5, as said below
- station_pairs: int32 [512, 2], replicated, may hold values from 0 to 191, as said below
- average_bands: int32 [512, 2], replicated, may hold values from 0 to 3, as said below
- tile_map: int32 [512, 32], replicated, may hold values from 0 to 255
- baseline_order: int32 [512], replicated, may hold values from 0 to 511, as said below
Outputs:
- averaged: bfloat16 [32, 8, 512, 1024], P(None, None, 'tm', 'chan')
- gridded: float32 [256, 8, 1024], P('tm', None, 'chan')
Inputs may be any that keep to these rules, and one draw needn't show every extreme that they name: `station_pairs`: row b holds the two stations of baseline b, the first smaller than the second. `average_bands`: column 0 is at most 3, column 1 at most 2. In each aligned block of 16 positions k of baseline_order, the bands of the baselines baseline_order[k] are, in some order, the pairs (3 - j % (3 + 1), 2 - j % (2 + 1)) for j = 0 to 15. `baseline_order`: each baseline once. `station_gains`: diagonal Jones entries have magnitudes of order one.
All inputs are finite; a program needn't handle non-finite values.
Results may differ from a plain program's by a relative error of at most 0.019.
Values may be sent and summed in bfloat16 or wider, within the bound.
No kernel may reach another device: no remote copies, remote signals or barrier semaphores. Data moves between devices by JAX's collectives and lax.ppermute only.
A program may use at most 128 MiB of HBM per device.

v0:
```python
import jax
import jax.numpy as jnp
from jax import lax
from jax.sharding import PartitionSpec as P

TILE_DEV = 8
TLOG = 3
CLOG = 2


def product(left, right):
    return (left[0] * right[0] - left[1] * right[1], left[0] * right[1] + left[1] * right[0])


def product_conj(left, right):
    return (left[0] * right[0] + left[1] * right[1], left[1] * right[0] - left[0] * right[1])


def add_pair(left, right):
    return (left[0] + right[0], left[1] + right[1])


def as_matrix(components):
    return [
        [(components[0], components[1]), (components[2], components[3])],
        [(components[4], components[5]), (components[6], components[7])],
    ]


def jones_apply(first, middle, second):
    left_gain = as_matrix(first)
    coherency = as_matrix(middle)
    right_gain = as_matrix(second)
    partial_rows = [
        [
            add_pair(
                product(left_gain[i][0], coherency[0][k]), product(left_gain[i][1], coherency[1][k])
            )
            for k in range(2)
        ]
        for i in range(2)
    ]
    result = []
    for i in range(2):
        for c in range(2):
            element = add_pair(
                product_conj(partial_rows[i][0], right_gain[c][0]),
                product_conj(partial_rows[i][1], right_gain[c][1]),
            )
            result.extend(element)
    return result


def calibrate(samples, gain_table, first_station, second_station):
    left_gain = jnp.take(gain_table, first_station, axis=1)
    right_gain = jnp.take(gain_table, second_station, axis=1)
    values = [samples[:, i].astype(jnp.float32) for i in range(8)]
    result = jones_apply(
        [left_gain[i][None] for i in range(8)], values, [right_gain[i][None] for i in range(8)]
    )
    return jnp.stack(result, axis=1).astype(jnp.bfloat16)


def halve_time(current, size):
    extent = current.shape[0]
    shaped = current.reshape((extent // size, 2, size // 2) + current.shape[1:])
    merged = 0.5 * (shaped[:, 0:1] + shaped[:, 1:2])
    return jnp.broadcast_to(merged, shaped.shape).reshape(current.shape)


def halve_chan(current, size):
    extent = current.shape[-1]
    shaped = current.reshape(current.shape[:-1] + (extent // size, 2, size // 2))
    merged = 0.5 * (shaped[..., 0:1, :] + shaped[..., 1:2, :])
    return jnp.broadcast_to(merged, shaped.shape).reshape(current.shape)


def band_average(samples, time_levels, chan_levels):
    values = samples.astype(jnp.float32)
    time_select = time_levels[None, None, :, None]
    chan_select = chan_levels[None, None, :, None]
    result = values
    current = values
    for k in range(1, TLOG + 1):
        current = halve_time(current, 2**k)
        result = jnp.where(time_select >= k, current, result)
    final = result
    current = result
    for k in range(1, CLOG + 1):
        current = halve_chan(current, 2**k)
        final = jnp.where(chan_select >= k, current, final)
    return final.astype(jnp.bfloat16)


def shards(visibilities, station_gains, station_pairs, average_bands, tile_map, baseline_order):
    chan_width = visibilities.shape[3]
    block_size = visibilities.shape[2] // lax.axis_size("tm")
    all_gains = lax.all_gather(station_gains, "chan", axis=1, tiled=True)
    gain_table = lax.dynamic_slice_in_dim(
        all_gains, lax.axis_index("chan") * chan_width, chan_width, 2
    )
    reordered = jnp.take(visibilities, baseline_order, axis=2)
    rows_here = lax.dynamic_slice_in_dim(
        baseline_order, lax.axis_index("tm") * block_size, block_size
    )
    bands_here = average_bands[rows_here]
    ordered_pairs = station_pairs[baseline_order]
    payload = calibrate(reordered, gain_table, ordered_pairs[:, 0], ordered_pairs[:, 1])
    turned = lax.all_to_all(payload, "tm", split_axis=2, concat_axis=0, tiled=True)
    averaged = band_average(turned, bands_here[:, 0], bands_here[:, 1])
    tile_here = tile_map[rows_here].T
    time_index = jnp.arange(averaged.shape[0], dtype=jnp.int32)[:, None]
    period = jnp.left_shift(jnp.ones_like(bands_here[:, 0]), bands_here[:, 0])[None, :]
    tile_ids = jnp.where(time_index % period == 0, tile_here, -1)
    targets = jnp.arange(TILE_DEV * lax.axis_size("tm"), dtype=jnp.int32)
    one_hot = (tile_ids[None] == targets[:, None, None]).astype(jnp.bfloat16)
    gridded = lax.psum_scatter(
        jnp.einsum("rtb,tkbc->rkc", one_hot, averaged, preferred_element_type=jnp.float32).astype(
            jnp.bfloat16
        ),
        "tm",
        scatter_dimension=0,
        tiled=True,
    ).astype(jnp.float32)
    return (averaged, gridded)


def solution(mesh):
    return jax.shard_map(
        shards,
        mesh=mesh,
        in_specs=(P("tm", None, None, "chan"), P(None, "chan", None), P(), P(), P(), P()),
        out_specs=(P(None, None, "tm", "chan"), P("tm", None, "chan")),
        check_vma=False,
    )
```

profile of v0, /device:TPU:8, one launch (start us, length us, event | category | flops | bytes accessed | tf_op | source)
XLA Modules:
  0.0 475.1 jit_solution(13990417689148985308)
XLA Ops:
  7.2 2.5 copy.586
  9.8 0.1 copy.585
  10.0 0.7 copy.639
  10.7 1.0 gather_fusion.1
  11.8 1.8 gather_fusion.2
  13.6 0.3 slice_reduce_fusion
  13.9 0.2 bitcast_select_fusion.1
  14.1 41.8 %all-gather.2.cloned.1.call-done = f32[8,192,1024]{2,0,1:T(8,128)} async-done(((f32[8,24,1024]{2,0,1:T(8,128)}), f32[8,192,1024]{2,0,1:T(8,128)}) %all-gather.2.cloned.1.call-update) | async-done | bytes 6291472 | tf_op jit(solution)/shard_map/all_gather | solution.py:98
  55.9 1.2 constant_dynamic-slice_fusion
  57.1 2.7 gather_fusion.5
  59.8 2.7 gather_fusion.4
  62.5 2.2 fusion.11
  64.8 0.5 fusion.12
  65.3 0.4 bitcast_dynamic-update-slice_fusion.7
  66.0 0.4 bitcast_dynamic-update-slice_fusion.3
  66.8 1.6 copy.591
  68.5 9.8 %all-to-all-start = ((bf16[1,8,512,128]{3,1,0,2:T(8,128)(2,1)}), bf16[1,8,512,128]{3,1,0,2:T(8,128)(2,1)S(1)}, u32[]{:S(2)}, u32[]{:S(2)}) async-start(bf16[1,8,512,128]{3,1,0,2:T(8,128)(2,1)} %copy.591), calls=%async_computation | async-start | bytes 2097152 | tf_op jit(solution)/shard_map/all_to_all | solution.py:109
  78.4 0.1 copy.584
  78.7 0.6 gather_fusion
  79.3 0.6 gather_fusion.3
  80.0 0.8 compare_reduce_fusion.4
  80.8 0.2 bitcast_select_fusion.2
  81.0 26.3 %all-to-all-done = bf16[1,8,512,128]{3,1,0,2:T(8,128)(2,1)S(1)} async-done(((bf16[1,8,512,128]{3,1,0,2:T(8,128)(2,1)}), bf16[1,8,512,128]{3,1,0,2:T(8,128)(2,1)S(1)}, u32[]{:S(2)}, u32[]{:S(2)}) %all-to-all-start) | async-done | bytes 1048608 | tf_op jit(solution)/shard_map/all_to_all | solution.py:109
  107.3 0.1 copy.592
  107.4 1.6 convert_bitcast_fusion
  109.0 0.2 convert.65
  109.2 1.1 fusion.59
  110.6 2.8 copy.621
  113.3 2.6 copy.620
  116.0 5.8 %add_multiply_fusion = f32[8,1,8,16,128]{3,2,4,0,1:T(8,128)} fusion(f32[8,1,8,16,128]{3,2,4,0,1:T(8,128)} %copy.620, f32[8,1,8,16,128]{3,2,4,0,1:T(8,128)} %copy.621), kind=kLoop, calls=%fused_computation.7 | loop fusion | flops 262144 | bytes 1572864 | tf_op jit(solution)/shard_map/mul | solution.py:67
  121.8 2.7 copy.625
  124.5 2.4 fusion.5
  126.9 0.6 copy.624
  127.6 6.6 %copy.598 = f32[32,1,8,16,128]{0,3,4,2,1:T(8,128)} copy(f32[32,1,8,16,128]{4,3,0,2,1:T(8,128)} %convert_bitcast_fusion) | data formatting | bytes 4194304 | tf_op jit(solution)/shard_map/convert_element_type | solution.py:79
  134.2 8.7 %copy.600 = f32[32,8,16,64,2,1]{3,2,5,4,1,0:T(8,128)} copy(f32[32,8,16,64,2,1]{0,2,4,3,1,5:T(8,128)} %bitcast.225) | data formatting | bytes 4194304 | tf_op jit(solution)/shard_map/convert_element_type | solution.py:79
  142.9 6.0 %copy.597 = f32[16,8,16,128]{2,1,3,0:T(8,128)} copy(f32[16,8,16,128]{3,2,0,1:T(8,128)} %fusion.59) | data formatting | bytes 2097152 | tf_op jit(solution)/shard_map/broadcast_in_dim | solution.py:68
  148.9 11.0 %broadcast_in_dim.122 = f32[16,2,8,16,128]{3,2,4,1,0:T(8,128)} broadcast(f32[16,8,16,128]{2,1,3,0:T(8,128)} %copy.597), dimensions={0,2,3,4} | broadcast | bytes 3145728 | tf_op jit(solution)/shard_map/broadcast_in_dim | solution.py:68
  159.9 11.9 %copy.599 = f32[32,8,16,64,2,1]{3,2,5,4,1,0:T(8,128)} copy(f32[32,8,16,64,2,1]{2,1,4,3,0,5:T(8,128)} %bitcast.219) | data formatting | bytes 4194304 | tf_op jit(solution)/shard_map/broadcast_in_dim | solution.py:68
  171.8 7.6 %broadcast_in_dim.117 = f32[4,2,4,8,16,128]{4,3,5,2,1,0:T(8,128)} broadcast(f32[4,8,16,128]{2,1,3,0:T(8,128)S(1)} %fusion.5), dimensions={0,3,4,5} | broadcast | bytes 2359296 | tf_op jit(solution)/shard_map/broadcast_in_dim | solution.py:68
  179.4 12.0 %copy.602 = f32[32,8,16,64,2,1]{3,2,5,4,1,0:T(8,128)} copy(f32[32,8,16,64,2,1]{2,1,4,3,0,5:T(8,128)} %bitcast.220) | data formatting | bytes 4194304 | tf_op jit(solution)/shard_map/reshape | solution.py:68
  191.4 10.2 %broadcast_in_dim.119 = f32[8,2,2,8,16,128]{4,3,5,2,1,0:T(8,128)} broadcast(f32[8,8,16,128]{2,1,3,0:T(8,128)} %bitcast.224), dimensions={0,3,4,5} | broadcast | bytes 2621440 | tf_op jit(solution)/shard_map/broadcast_in_dim | solution.py:68
  201.6 11.9 %copy.601 = f32[32,8,16,64,2,1]{3,2,5,4,1,0:T(8,128)} copy(f32[32,8,16,64,2,1]{2,1,4,3,0,5:T(8,128)} %bitcast.221) | data formatting | bytes 4194304 | tf_op jit(solution)/shard_map/reshape | solution.py:68
  213.5 8.0 %select_select_fusion = f32[32,8,16,64,2,1]{3,2,5,4,1,0:T(8,128)S(1)} fusion(f32[32,8,16,64,2,1]{3,2,5,4,1,0:T(8,128)} %copy.602, f32[32,8,16,64,2,1]{3,2,5,4,1,0:T(8,128)} %copy.601, f32[32,8,16,64,2,1]{3,2,5,4,1,0:T(8,128)} %copy.599, f32[32,8,16,64,2,1]{3,2,5,4,1,0:T(8,128)} %copy.600, pred[16]{0:T(512)(128)(4,1)S(1)} %get-tuple-element.31, ...), kind=kLoop, calls=%fused_computation.6 | loop fusion | flops 1572864 | bytes 10485808 | tf_op jit(solution)/shard_map/jit(_where)/select_n | solution.py:86
  221.6 1.7 fusion.58
  223.3 0.4 fusion.2
  223.6 4.5 copy.606
  228.2 4.1 broadcast_in_dim.128
  232.3 6.1 %copy.610 = bf16[32,8,16,128]{3,2,0,1:T(8,128)(2,1)} copy(bf16[32,8,16,128]{0,2,3,1:T(8,128)(2,1)} %bitcast.228) | data formatting | bytes 2097152 | tf_op jit(solution)/shard_map/broadcast_in_dim | solution.py:75
  238.4 3.6 copy.603
  242.0 2.5 fusion.1
  244.5 2.5 broadcast_in_dim.125
  247.0 6.2 %copy.611 = bf16[32,8,16,128]{3,2,0,1:T(8,128)(2,1)} copy(bf16[32,8,16,128]{0,2,3,1:T(8,128)(2,1)} %bitcast.230) | data formatting | bytes 2097152 | tf_op jit(solution)/shard_map/reshape | solution.py:75
  253.2 0.1 broadcast_in_dim.122.clone
  253.4 0.1 broadcast_in_dim.119.clone
  253.5 0.1 broadcast_in_dim.117.clone
  253.7 0.8 copy-done.2
  254.4 0.3 copy-done.3
  254.8 1.0 fusion.10
  255.7 0.6 fusion.14
  256.3 0.9 copy.640
  257.3 1.3 copy.614
  258.5 208.4 %reduce-scatter.4.cloned.1.call-done = bf16[8,1024]{1,0:T(8,128)(2,1)} async-done(((bf16[256,1024]{1,0:T(8,128)(2,1)}), bf16[8,1024]{1,0:T(8,128)(2,1)}) %reduce-scatter.4.cloned.1.call-update) | async-done | bytes 16400
  466.9 0.7 bitcast_convert_fusion
  467.6 0.6 copy.615
  (49 shorter events, 1.5 us)
Async XLA Ops:
  7.2 2.7 copy-start.9
  7.2 2.8 copy-start.4
  7.2 3.5 copy-start.6
  7.2 48.7 %all-gather.2.cloned.1.call-start = ((), (), s32[]{:S(2)}) async-start(), calls=%async_computation.2 | async-start | bytes 7077888 | tf_op jit(solution)/shard_map/all_gather | solution.py:98
  62.5 2.2 copy-start.1
  66.8 11.6 %copy-start.10 = (s32[512,2]{0,1:T(2,128)S(1)}, s32[512,2]{0,1:T(2,128)}, u32[]{:S(2)}) copy-start(s32[512,2]{0,1:T(2,128)} %param.11) | copy-start | bytes 12292
  66.8 11.7 %copy-start.5 = (s32[512,32]{0,1:T(8,128)S(1)}, s32[512,32]{0,1:T(8,128)}, u32[]{:S(2)}) copy-start(s32[512,32]{0,1:T(8,128)} %param.12) | copy-start | bytes 196612
  68.5 38.8 %all-to-all-start = ((bf16[1,8,512,128]{3,1,0,2:T(8,128)(2,1)}), bf16[1,8,512,128]{3,1,0,2:T(8,128)(2,1)S(1)}, u32[]{:S(2)}, u32[]{:S(2)}) async-start(bf16[1,8,512,128]{3,1,0,2:T(8,128)(2,1)} %copy.591), calls=%async_computation | async-start | bytes 2097152 | tf_op jit(solution)/shard_map/all_to_all | solution.py:109
  78.3 388.6 %reduce-scatter.4.cloned.1.call-start = ((), (), s32[]{:S(2)}) async-start(), calls=%async_computation.3 | async-start | bytes 540672
  201.6 11.9 %copy-start.7 = (pred[16]{0:T(512)(128)(4,1)S(1)}, pred[16]{0:T(512)(128)(4,1)}, u32[]{:S(2)}) copy-start(pred[16]{0:T(512)(128)(4,1)} %get-tuple-element.33) | copy-start | bytes 52
  247.0 6.2 %copy-start = (f32[16,8,16,128]{3,2,0,1:T(8,128)S(1)}, f32[16,8,16,128]{3,2,0,1:T(8,128)}, u32[]{:S(2)}) copy-start(f32[16,8,16,128]{3,2,0,1:T(8,128)} %fusion.59) | copy-start | bytes 3145732
  253.2 1.2 copy-start.2
  253.2 1.5 copy-start.3
  253.2 1.5 copy-start.8
  253.2 1.5 copy-start.11
  253.2 1.5 copy-start.12
Sparse Core Ops, SparseCore 0:
  10.4 45.4 all-gather.1
  257.4 209.4 reduce-scatter.3
where the time goes:
time: 476 us; the launch traced here: 475 us
  waiting for transfers between devices  276 us (58%)
  local copies, waits for them, and re-layouts  142 us (30%)
  other arithmetic  31.2 us (7%)
  between operations  14.4 us (3%)
  starting transfers between devices  9.9 us (2%)
    unnamed x3, waiting for transfers between devices  208 us
    broadcast_in_dim x8, local copies, waits for them, and re-layouts, halve_time(): return jnp.broadcast_to(merged, shaped.shape).reshape(current.shape)  47.1 us
    all_gather x1, waiting for transfers between devices, shards(): all_gains = lax.all_gather(station_gains, 'chan', axis=1, tiled=True)  41.8 us
    all_to_all x1, waiting for transfers between devices, shards(): lax.all_to_all(payload, 'tm', split_axis=2, concat_axis=0, tiled=True)  26.3 us
    reshape x2, local copies, waits for them, and re-layouts, halve_time(): return jnp.broadcast_to(merged, shaped.shape).reshape(current.shape)  23.9 us
    broadcast_in_dim x4, local copies, waits for them, and re-layouts, halve_chan(): return jnp.broadcast_to(merged, shaped.shape).reshape(current.shape)  17.2 us
    unnamed x38, local copies, waits for them, and re-layouts  16.4 us
    convert_element_type x2, local copies, waits for them, and re-layouts, band_average(): values = samples.astype(jnp.float32)  15.3 us
  transfers between devices with their start and end apart: 3, of which 3 were waited for; matrix products, arithmetic and copies ran while one was open for 2% of the time, Pallas kernels for 0%

commit v1 on v0

--- a/solution.py
+++ b/solution.py
@@ -106,7 +106,10 @@
     bands_here = average_bands[rows_here]
     ordered_pairs = station_pairs[baseline_order]
     payload = calibrate(reordered, gain_table, ordered_pairs[:, 0], ordered_pairs[:, 1])
-    turned = lax.all_to_all(payload, "tm", split_axis=2, concat_axis=0, tiled=True)
+    turned = jnp.concatenate(
+        lax.all_to_all(jnp.stack(jnp.split(payload, lax.axis_size("tm"), axis=2)), "tm", 0, 0),
+        axis=0,
+    )
     averaged = band_average(turned, bands_here[:, 0], bands_here[:, 1])
     tile_here = tile_map[rows_here].T
     time_index = jnp.arange(averaged.shape[0], dtype=jnp.int32)[:, None]

time: 476 us -> 491 us (1.032)
  local copies, waits for them, and re-layouts: 142 us -> 157 us
    unnamed x38 -> x62, local copies, waits for them, and re-layouts: 16.4 us -> 32.9 us
    broadcast_in_dim x8 -> x5, local copies, waits for them, and re-layouts: 47.1 us -> 46.7 us  [halve_time(): return jnp.broadcast_to(merged, shaped.shape).reshape(current.shape)]
  transfers between devices with their start and end apart: 3 -> 3, of which waited for: 3 -> 3; matrix products, arithmetic and copies ran while one was open for 2% -> 1% of each run, Pallas kernels for 0% -> 0%
where the time goes in v1:
time: 491 us; the launch traced here: 490 us
  waiting for transfers between devices  277 us (56%)
  local copies, waits for them, and re-layouts  157 us (32%)
  other arithmetic  30.8 us (6%)
  between operations  14.4 us (3%)
  starting transfers between devices  10.1 us (2%)
    unnamed x3, waiting for transfers between devices  209 us
    broadcast_in_dim x5, local copies, waits for them, and re-layouts, halve_time(): return jnp.broadcast_to(merged, shaped.shape).reshape(current.shape)  46.7 us
    all_gather x1, waiting for transfers between devices, shards(): all_gains = lax.all_gather(station_gains, 'chan', axis=1, tiled=True)  41.8 us
    unnamed x62, local copies, waits for them, and re-layouts  32.9 us
    all_to_all x1, waiting for transfers between devices, shards(): lax.all_to_all(jnp.stack(jnp.split(payload, lax.axis_size('tm'), axis=2))...  26.1 us
    reshape x2, local copies, waits for them, and re-layouts, halve_time(): return jnp.broadcast_to(merged, shaped.shape).reshape(current.shape)  23.9 us
    broadcast_in_dim x4, local copies, waits for them, and re-layouts, halve_chan(): return jnp.broadcast_to(merged, shaped.shape).reshape(current.shape)  17.5 us
    convert_element_type x2, local copies, waits for them, and re-layouts, band_average(): values = samples.astype(jnp.float32)  13.8 us
  transfers between devices with their start and end apart: 3, of which 3 were waited for; matrix products, arithmetic and copies ran while one was open for 1% of the time, Pallas kernels for 0%

profile of v1, /device:TPU:8, one launch (start us, length us, event | category | flops | bytes accessed | tf_op | source)
XLA Modules:
  0.0 489.9 jit_solution(18378595434833308072)
XLA Ops:
  7.2 2.5 copy.605
  10.0 0.7 copy.655
  10.7 1.0 gather_fusion.1
  11.8 1.8 gather_fusion.2
  14.1 41.8 %all-gather.2.cloned.1.call-done = f32[8,192,1024]{2,0,1:T(8,128)} async-done(((f32[8,24,1024]{2,0,1:T(8,128)}), f32[8,192,1024]{2,0,1:T(8,128)}) %all-gather.2.cloned.1.call-update) | async-done | bytes 6291472 | tf_op jit(solution)/shard_map/all_gather | solution.py:98
  55.9 1.2 constant_dynamic-slice_fusion
  57.1 2.7 gather_fusion.5
  59.9 2.7 gather_fusion.4
  62.5 2.2 fusion.11
  66.8 0.6 constant_dynamic-update-slice_fusion.31
  67.4 0.6 constant_dynamic-update-slice_fusion.30
  68.1 0.6 constant_dynamic-update-slice_fusion.29
  68.7 0.6 constant_dynamic-update-slice_fusion.28
  69.3 0.6 constant_dynamic-update-slice_fusion.27
  69.9 0.6 constant_dynamic-update-slice_fusion.26
  70.5 0.6 constant_dynamic-update-slice_fusion.25
  71.2 0.6 constant_dynamic-update-slice_fusion.24
  71.8 0.6 constant_dynamic-update-slice_fusion.23
  72.4 0.6 constant_dynamic-update-slice_fusion.22
  73.0 0.6 constant_dynamic-update-slice_fusion.21
  73.6 0.6 constant_dynamic-update-slice_fusion.20
  74.3 0.6 constant_dynamic-update-slice_fusion.19
  74.9 0.6 constant_dynamic-update-slice_fusion.18
  75.5 0.6 constant_dynamic-update-slice_fusion.17
  76.1 0.6 constant_dynamic-update-slice_fusion.16
  76.7 0.6 constant_dynamic-update-slice_fusion.15
  78.6 0.6 constant_dynamic-update-slice_fusion.12
  79.2 0.6 constant_dynamic-update-slice_fusion.11
  81.1 0.6 constant_dynamic-update-slice_fusion.8
  82.9 0.6 constant_dynamic-update-slice_fusion.5
  84.8 0.6 constant_dynamic-update-slice_fusion.2
  86.6 9.8 %all-to-all-start = ((bf16[32,1,8,16,128]{4,3,2,1,0:T(8,128)(2,1)}), bf16[32,1,8,16,128]{4,3,2,1,0:T(8,128)(2,1)S(1)}, u32[]{:S(2)}, u32[]{:S(2)}) async-start(bf16[32,1,8,16,128]{4,3,2,1,0:T(8,128)(2,1)} %constant_dynamic-update-slice_fusion), calls=%async_computation | async-start | bytes 2097152 | tf_op jit(solution)/shard_map/all_to_all | solution.py:110
  98.3 0.8 compare_reduce_fusion.4
  99.3 26.1 %all-to-all-done = bf16[32,1,8,16,128]{4,3,2,1,0:T(8,128)(2,1)S(1)} async-done(((bf16[32,1,8,16,128]{4,3,2,1,0:T(8,128)(2,1)}), bf16[32,1,8,16,128]{4,3,2,1,0:T(8,128)(2,1)S(1)}, u32[]{:S(2)}, u32[]{:S(2)}) %all-to-all-start) | async-done | bytes 1048608 | tf_op jit(solution)/shard_map/all_to_all | solution.py:110
  125.7 1.1 fusion.59
  127.1 2.6 copy.637
  129.7 2.6 copy.636
  132.3 5.8 %add_multiply_fusion = f32[8,1,8,16,128]{3,2,4,0,1:T(8,128)} fusion(f32[8,1,8,16,128]{3,2,4,0,1:T(8,128)} %copy.636, f32[8,1,8,16,128]{3,2,4,0,1:T(8,128)} %copy.637), kind=kLoop, calls=%fused_computation.7 | loop fusion | flops 262144 | bytes 1572864 | tf_op jit(solution)/shard_map/mul | solution.py:67
  138.2 2.6 copy.641
  140.8 2.4 fusion.5
  143.7 6.0 %copy.614 = f32[16,8,16,128]{2,1,3,0:T(8,128)} copy(f32[16,8,16,128]{3,2,1,0:T(8,128)} %fusion.59) | data formatting | bytes 2097152 | tf_op jit(solution)/shard_map/broadcast_in_dim | solution.py:68
  149.7 11.0 %broadcast_in_dim.122 = f32[16,2,8,16,128]{3,2,4,1,0:T(8,128)} broadcast(f32[16,8,16,128]{2,1,3,0:T(8,128)} %copy.614), dimensions={0,2,3,4} | broadcast | bytes 3145728 | tf_op jit(solution)/shard_map/broadcast_in_dim | solution.py:68
  160.7 12.0 %copy.616 = f32[32,8,16,64,2,1]{3,2,5,4,1,0:T(8,128)} copy(f32[32,8,16,64,2,1]{2,1,4,3,0,5:T(8,128)} %bitcast.344) | data formatting | bytes 4194304 | tf_op jit(solution)/shard_map/broadcast_in_dim | solution.py:68
  172.6 5.1 %copy.615 = f32[32,1,8,16,128]{0,3,4,2,1:T(8,128)} copy(bf16[32,1,8,16,128]{4,3,2,1,0:T(8,128)(2,1)S(1)} %all-to-all-done) | data formatting | bytes 3145728 | tf_op jit(solution)/shard_map/convert_element_type | solution.py:79
  177.7 8.7 %copy.617 = f32[32,8,16,64,2,1]{3,2,5,4,1,0:T(8,128)} copy(f32[32,8,16,64,2,1]{0,2,4,3,1,5:T(8,128)} %bitcast.350) | data formatting | bytes 4194304 | tf_op jit(solution)/shard_map/convert_element_type | solution.py:79
  186.4 7.6 %broadcast_in_dim.117 = f32[4,2,4,8,16,128]{4,3,5,2,1,0:T(8,128)} broadcast(f32[4,8,16,128]{2,1,3,0:T(8,128)S(1)} %fusion.5), dimensions={0,3,4,5} | broadcast | bytes 2359296 | tf_op jit(solution)/shard_map/broadcast_in_dim | solution.py:68
  194.0 11.9 %copy.619 = f32[32,8,16,64,2,1]{3,2,5,4,1,0:T(8,128)} copy(f32[32,8,16,64,2,1]{2,1,4,3,0,5:T(8,128)} %bitcast.345) | data formatting | bytes 4194304 | tf_op jit(solution)/shard_map/reshape | solution.py:68
  206.0 10.2 %broadcast_in_dim.119 = f32[8,2,2,8,16,128]{4,3,5,2,1,0:T(8,128)} broadcast(f32[8,8,16,128]{2,1,3,0:T(8,128)} %bitcast.349), dimensions={0,3,4,5} | broadcast | bytes 2621440 | tf_op jit(solution)/shard_map/broadcast_in_dim | solution.py:68
  216.2 11.9 %copy.618 = f32[32,8,16,64,2,1]{3,2,5,4,1,0:T(8,128)} copy(f32[32,8,16,64,2,1]{2,1,4,3,0,5:T(8,128)} %bitcast.346) | data formatting | bytes 4194304 | tf_op jit(solution)/shard_map/reshape | solution.py:68
  228.1 8.0 %select_select_fusion = f32[32,8,16,64,2,1]{3,2,5,4,1,0:T(8,128)S(1)} fusion(f32[32,8,16,64,2,1]{3,2,5,4,1,0:T(8,128)} %copy.619, f32[32,8,16,64,2,1]{3,2,5,4,1,0:T(8,128)} %copy.618, f32[32,8,16,64,2,1]{3,2,5,4,1,0:T(8,128)} %copy.616, f32[32,8,16,64,2,1]{3,2,5,4,1,0:T(8,128)} %copy.617, pred[16]{0:T(512)(128)(4,1)S(1)} %get-tuple-element.31, ...), kind=kLoop, calls=%fused_computation.6 | loop fusion | flops 1572864 | bytes 10485808 | tf_op jit(solution)/shard_map/jit(_where)/select_n | solution.py:86
  236.2 1.7 fusion.58
  238.3 4.5 copy.623
  242.8 4.1 broadcast_in_dim.128
  246.9 6.4 %copy.627 = bf16[32,8,16,128]{3,2,1,0:T(8,128)(2,1)} copy(bf16[32,8,16,128]{0,2,3,1:T(8,128)(2,1)} %bitcast.353) | data formatting | bytes 2097152 | tf_op jit(solution)/shard_map/broadcast_in_dim | solution.py:75
  253.3 3.6 copy.620
  256.9 2.5 fusion.1
  259.4 2.5 broadcast_in_dim.125
  261.9 6.6 %copy.628 = bf16[32,8,16,128]{3,2,1,0:T(8,128)(2,1)} copy(bf16[32,8,16,128]{0,2,3,1:T(8,128)(2,1)} %bitcast.355) | data formatting | bytes 2097152 | tf_op jit(solution)/shard_map/reshape | solution.py:75
  268.5 2.0 fusion.10
  270.5 0.9 fusion.14
  271.5 0.9 copy.656
  272.4 209.3 %reduce-scatter.4.cloned.1.call-done = bf16[8,1024]{1,0:T(8,128)(2,1)} async-done(((bf16[256,1024]{1,0:T(8,128)(2,1)}), bf16[8,1024]{1,0:T(8,128)(2,1)}) %reduce-scatter.4.cloned.1.call-update) | async-done | bytes 16400
  481.8 0.7 bitcast_convert_fusion
  482.5 0.6 copy.631
  (68 shorter events, 12.5 us)
Async XLA Ops:
  7.2 2.7 copy-start.8
  7.2 2.8 copy-start.3
  7.2 3.5 copy-start.6
  7.2 48.7 %all-gather.2.cloned.1.call-start = ((), (), s32[]{:S(2)}) async-start(), calls=%async_computation.2 | async-start | bytes 7077888 | tf_op jit(solution)/shard_map/all_gather | solution.py:98
  62.5 2.2 copy-start.1
  66.8 29.9 %copy-start.9 = (s32[512,2]{0,1:T(2,128)S(1)}, s32[512,2]{0,1:T(2,128)}, u32[]{:S(2)}) copy-start(s32[512,2]{0,1:T(2,128)} %param.11) | copy-start | bytes 12292
  69.3 27.6 %copy-start.5 = (s32[512,32]{0,1:T(8,128)S(1)}, s32[512,32]{0,1:T(8,128)}, u32[]{:S(2)}) copy-start(s32[512,32]{0,1:T(8,128)} %param.12) | copy-start | bytes 196612
  86.6 38.8 %all-to-all-start = ((bf16[32,1,8,16,128]{4,3,2,1,0:T(8,128)(2,1)}), bf16[32,1,8,16,128]{4,3,2,1,0:T(8,128)(2,1)S(1)}, u32[]{:S(2)}, u32[]{:S(2)}) async-start(bf16[32,1,8,16,128]{4,3,2,1,0:T(8,128)(2,1)} %constant_dynamic-update-slice_fusion), calls=%async_computation | async-start | bytes 2097152 | tf_op jit(solution)/shard_map/all_to_all | solution.py:110
  96.5 385.3 %reduce-scatter.4.cloned.1.call-start = ((), (), s32[]{:S(2)}) async-start(), calls=%async_computation.3 | async-start | bytes 540672
  216.2 11.9 %copy-start.7 = (pred[16]{0:T(512)(128)(4,1)S(1)}, pred[16]{0:T(512)(128)(4,1)}, u32[]{:S(2)}) copy-start(pred[16]{0:T(512)(128)(4,1)} %get-tuple-element.33) | copy-start | bytes 52
  261.9 6.6 %copy-start = (f32[16,8,16,128]{3,2,1,0:T(8,128)S(1)}, f32[16,8,16,128]{3,2,1,0:T(8,128)}, u32[]{:S(2)}) copy-start(f32[16,8,16,128]{3,2,1,0:T(8,128)} %fusion.59) | copy-start | bytes 3145732
  261.9 6.6 %copy-start.2 = (bf16[32,8,16,128]{3,2,1,0:T(8,128)(2,1)S(1)}, bf16[32,8,16,128]{3,2,1,0:T(8,128)(2,1)}, u32[]{:S(2)}) copy-start(bf16[32,8,16,128]{3,2,1,0:T(8,128)(2,1)} %copy.627) | copy-start | bytes 3145732
  270.5 1.0 copy-start.4
Sparse Core Ops, SparseCore 0:
  10.4 45.4 all-gather.1
  272.6 209.1 reduce-scatter.3
